TPU v7x, 128 devices: a whole 4x4x4 slice. The times are simulated.
128 devices in a mesh: side: 2 (over y_lo), grp: 8 (over y_hi, z), cuts: 8 (over x, core).
Axes of the slice: x: 4, y: 4 (y_hi: 2, y_lo: 2; y = y_hi * 2 + y_lo), z: 4, core: 2. Of those that a mesh axis runs over, the one named last changes fastest.
Arguments:
- query: bfloat16 [512, 6144], P(('side', 'grp', 'cuts')), may hold values from -21 to 21, as said below
- k_cache: bfloat16 [512, 256, 1024], P(('side', 'grp', 'cuts')), may hold values from -5 to 5
- v_cache: bfloat16 [512, 256, 1024], P(('side', 'grp', 'cuts')), may hold values from -6 to 6
- new_key: bfloat16 [512, 1024], P(('side', 'grp', 'cuts')), may hold values from -6 to 6
- new_value: bfloat16 [512, 1024], P(('side', 'grp', 'cuts')), may hold values from -6 to 6
- lengths: int32 [512], P(('side', 'grp', 'cuts')), may hold values from 2 to 256, as said below
- residual: bfloat16 [512, 6144], P(('side', 'grp', 'cuts')), may hold values from -6 to 6
- norm_gain: bfloat16 [6144], replicated, may hold values from 0.099609375 to 1.8984375
- router: bfloat16 [6144, 8], replicated, may hold values from -0.078125 to 0.078125
- routes: int32 [512, 2], P(('side', 'grp', 'cuts')), may hold values from 0 to 7, all different within a row; in each aligned block of 4 rows (0 to 3, 4 to 7, ...) at most 2 rows name the same one
- w_gate: bfloat16 [8, 6144, 8192], P('grp', None, ('side', 'cuts')), may hold values from -0.078125 to 0.078125
- w_up: bfloat16 [8, 6144, 8192], P('grp', None, ('side', 'cuts')), may hold values from -0.078125 to 0.078125
- w_down: bfloat16 [8, 8192, 6144], P('grp', ('side', 'cuts')), may hold values from -0.0625 to 0.0625
Outputs:
- layer_out: bfloat16 [512, 6144], P(('side', 'grp', 'cuts'))
Inputs may be any that keep to these rules, and one draw needn't show every extreme that they name: `query`: queries are the new token's queries; in some draws a few rows have queries aligned with some cached keys. `lengths`: some row in every draw has all 256 positions live. `routes`: the two experts of a row differ. Within the rows of one device (aligned blocks of 4 rows) no expert is named more than 2 times, a bound that some block of every draw reaches.
All inputs are finite; a program needn't handle non-finite values.
Results may differ from a plain program's by a relative error of at most 0.0095.
Values may be sent and summed in bfloat16 or wider, within the bound.
A program may use at most 128 MiB of HBM per device.

v0:
```python
import math

import jax
import jax.numpy as jnp
from jax import lax
from jax.sharding import PartitionSpec as P

Q_HEADS = 48
KV_HEADS = 8
HEAD_DIM = 128


def attend(query, k_cache, v_cache, new_key, new_value, lengths):
    rows, span, _ = k_cache.shape
    group = Q_HEADS // KV_HEADS
    scale = 1.0 / math.sqrt(HEAD_DIM)
    queries = query.reshape(rows, KV_HEADS, group, HEAD_DIM)
    keys = k_cache.reshape(rows, span, KV_HEADS, HEAD_DIM)
    values = v_cache.reshape(rows, span, KV_HEADS, HEAD_DIM)
    fresh_key = new_key.reshape(rows, KV_HEADS, HEAD_DIM)
    fresh_value = new_value.astype(jnp.float32).reshape(rows, KV_HEADS, 1, HEAD_DIM)
    old = jnp.einsum("rkgd,rskd->rkgs", queries, keys, preferred_element_type=jnp.float32) * scale
    own = (
        jnp.einsum("rkgd,rkd->rkg", queries, fresh_key, preferred_element_type=jnp.float32) * scale
    )
    live = jnp.arange(span)[None, :] < lengths[:, None]
    old = jnp.where(live[:, None, None, :], old, -jnp.inf)
    top = jnp.maximum(jnp.max(old, axis=-1), own)
    e_old = jnp.exp(old - top[..., None])
    e_own = jnp.exp(own - top)
    total = jnp.sum(e_old, axis=-1) + e_own
    p_old = (e_old / total[..., None]).astype(jnp.bfloat16)
    p_own = (e_own / total).astype(jnp.bfloat16).astype(jnp.float32)
    out = jnp.einsum("rkgs,rskd->rkgd", p_old, values, preferred_element_type=jnp.float32)
    out = out + p_own[..., None] * fresh_value
    return out.reshape(rows, Q_HEADS * HEAD_DIM)


def slot_ranks(block):
    flat = block.reshape(-1)
    order = jnp.arange(flat.shape[0])
    same = (flat[:, None] == flat[None, :]) & (order[None, :] < order[:, None])
    return jnp.sum(same.astype(jnp.int32), axis=1).reshape(block.shape)


def activate(rows_in, gate_w, up_w):
    gate = jnp.dot(rows_in, gate_w, preferred_element_type=jnp.float32)
    upper = jnp.dot(rows_in, up_w, preferred_element_type=jnp.float32)
    return (jax.nn.silu(gate) * upper).astype(jnp.bfloat16)


def local(
    query,
    k_cache,
    v_cache,
    new_key,
    new_value,
    lengths,
    residual,
    norm_gain,
    router,
    routes,
    w_gate,
    w_up,
    w_down,
):
    rows = query.shape[0]
    width = query.shape[1]
    experts = lax.axis_size("grp")
    n_side = lax.axis_size("side")
    n_cuts = lax.axis_size("cuts")
    most = max(2, 2 * rows // experts)
    gate_w = w_gate[0]
    up_w = w_up[0]
    down_w = w_down[0]
    attended = attend(query, k_cache, v_cache, new_key, new_value, lengths)
    mixed = residual.astype(jnp.float32) + attended
    power = jnp.mean(mixed * mixed, axis=1, keepdims=True)
    normed = (mixed * lax.rsqrt(power + 1e-05) * norm_gain.astype(jnp.float32)).astype(jnp.bfloat16)
    logits = jnp.dot(normed, router, preferred_element_type=jnp.float32)
    chosen = routes[:, :, None] == jnp.arange(experts)[None, None, :]
    picked = jnp.sum(jnp.where(chosen, logits[:, None, :], 0.0), axis=-1)
    first = jax.nn.sigmoid(picked[:, 0] - picked[:, 1])
    second = jax.nn.sigmoid(picked[:, 1] - picked[:, 0])
    weights = jnp.stack([first, second], axis=1)
    ranks = slot_ranks(routes)
    slot_of = routes * most + ranks
    slot_range = jnp.arange(experts * most)
    placing = slot_of[:, :, None] == slot_range[None, None, :]
    one_hot = jnp.sum(placing.astype(jnp.float32), axis=1).astype(jnp.bfloat16)
    outgoing = jnp.einsum("rj,rx->jx", one_hot, normed, preferred_element_type=jnp.float32).astype(
        jnp.bfloat16
    )
    copies = jnp.broadcast_to(
        outgoing.reshape(1, experts, 1, most, width), (n_side, experts, n_cuts, most, width)
    )
    arrived = lax.all_to_all(
        copies.reshape(-1, width), ("side", "grp", "cuts"), split_axis=0, concat_axis=0, tiled=True
    )
    hidden = activate(arrived, gate_w, up_w)
    ff_dev = hidden.shape[1]
    hidden = (
        hidden.reshape(n_side, experts, n_cuts, most, ff_dev)
        .transpose(0, 2, 1, 3, 4)
        .reshape(-1, ff_dev)
    )
    mine = lax.psum_scatter(
        jnp.dot(hidden, down_w, preferred_element_type=jnp.float32).astype(jnp.bfloat16),
        ("side", "cuts"),
        scatter_dimension=0,
        tiled=True,
    ).astype(jnp.float32)
    returned = lax.all_to_all(
        mine.astype(jnp.bfloat16), "grp", split_axis=0, concat_axis=0, tiled=True
    ).astype(mine.dtype)
    mixing = jnp.sum(jnp.where(placing, weights[:, :, None], 0.0), axis=1)
    combined = jnp.dot(
        mixing, returned, precision=lax.Precision.HIGHEST, preferred_element_type=jnp.float32
    )
    return (mixed + combined).astype(jnp.bfloat16)


def solution(mesh):
    placed = (
        P(("side", "grp", "cuts"), None),
        P(("side", "grp", "cuts"), None, None),
        P(("side", "grp", "cuts"), None, None),
        P(("side", "grp", "cuts"), None),
        P(("side", "grp", "cuts"), None),
        P(("side", "grp", "cuts")),
        P(("side", "grp", "cuts"), None),
        P(),
        P(),
        P(("side", "grp", "cuts"), None),
        P("grp", None, ("side", "cuts")),
        P("grp", None, ("side", "cuts")),
        P("grp", ("side", "cuts"), None),
    )
    return jax.shard_map(
        local,
        mesh=mesh,
        in_specs=placed,
        out_specs=P(("side", "grp", "cuts"), None),
        check_vma=False,
    )
```

profile of v0, /device:TPU:0, one launch (start us, length us, event | category | flops | bytes accessed | tf_op | source)
XLA Modules:
  0.0 181.6 jit_solution(13028045160434977673)
XLA Ops:
  6.5 0.0 copy-start
  6.5 0.0 reduce-scatter.2.cloned.1.call-start
  6.5 0.9 iota_compare_fusion.3
  7.4 0.8 copy.27
  8.2 0.1 eq.20
  8.3 0.2 convert_reduce_fusion.1
  8.5 0.1 reshape.74
  8.5 0.1 copy.29
  8.6 0.7 reshape.81
  9.4 0.7 convert_bitcast_fusion
  10.1 0.7 convert_element_type.48
  10.8 0.9 reshape.69
  11.6 0.1 fusion.35
  11.8 0.0 copy-done
  11.8 0.0 copy-start.2
  11.8 0.0 copy-start.4
  11.8 0.0 copy-start.3
  11.8 0.7 fusion.34
  12.6 0.2 fusion.27
  12.8 2.0 %fusion.24 = f32[4,8,6,128]{3,2,1,0:T(8,128)S(1)} fusion(f32[4,8,6,256]{3,2,1,0:T(8,128)S(1)} %get-tuple-element.12, f32[4,8,6]{2,1,0:T(8,128)S(1)} %get-tuple-element.8, f32[4,8,6]{2,1,0:T(8,128)S(1)} %multiply_maximum_fusion, f32[4,8,128]{2,1,0:T(8,128)S(1)} %bitcast.62, f32[4,8,6]{2,1,0:T(8,128)S(1)} %get-tuple-element.7, bf16[4,256,1024]{2,1,0:T(8,128)(2,1)} %param.15), kind=kOutput, calls=%fused_computation.19 | convolution fusion | flops 12779520 | bytes 2410752 | tf_op jit(solution)/shard_map/rkgs,rskd->rkgd/dot_general | solution.py:34
  14.9 0.1 reshape.73
  14.9 0.0 copy-done.2
  14.9 0.2 multiply_reduce_fusion
  15.1 0.1 multiply_convert_fusion
  15.2 0.0 copy-done.4
  15.2 0.2 fusion.36
  15.4 0.0 copy-done.3
  15.4 0.2 select_reduce_fusion.1
  15.6 0.1 convert_reduce_fusion
  15.7 0.3 convolution_convert_fusion.1
  15.9 0.1 broadcast_in_dim.65
  16.1 2.0 %broadcast_in_dim.66 = bf16[2,8,8,2,6144]{4,3,2,1,0:T(2,128)(2,1)S(1)} broadcast(bf16[8,2,6144]{2,1,0:T(2,128)(2,1)S(1)} %broadcast_in_dim.65), dimensions={1,3,4} | broadcast | bytes 3342336 | tf_op jit(solution)/shard_map/broadcast_in_dim | solution.py:94
  18.1 52.9 %all_to_all.24 = bf16[128,2,6144]{2,1,0:T(2,128)(2,1)} all-to-all(bf16[128,2,6144]{2,1,0:T(2,128)(2,1)S(1)} %bitcast.58), channel_id=1, replica_groups=mesh['side'=2,'grp'=8,'cuts'=8] {'side','grp','cuts'}, dimensions={0} | all-to-all | bytes 6291456 | tf_op jit(solution)/shard_map/all_to_all | solution.py:97
  71.0 7.3 %all_to_all.18 = bf16[256,6144]{1,0:T(8,128)(2,1)} reshape(bf16[128,2,6144]{2,1,0:T(2,128)(2,1)} %all_to_all.24) | data formatting | bytes 6291456 | tf_op jit(solution)/shard_map/all_to_all | solution.py:97
  78.4 0.0 copy-start.1
  78.4 5.7 %fusion.4 = f32[256,512]{1,0:T(8,128)S(1)} fusion(bf16[256,6144]{1,0:T(8,128)(2,1)} %all_to_all.18, bf16[1,6144,512]{2,1,0:T(8,128)(2,1)} %param.23), kind=kOutput, calls=%fused_computation.7 | convolution fusion | flops 1610612736 | bytes 9961472 | tf_op jit(solution)/shard_map/dot_general | solution.py:47
  84.0 0.0 copy-done.1
  84.0 4.7 %fusion.15 = bf16[256,512]{1,0:T(8,128)(2,1)S(1)} fusion(bf16[256,6144]{1,0:T(8,128)(2,1)S(1)} %copy-done.1, bf16[1,6144,512]{2,1,0:T(8,128)(2,1)} %param.24, f32[256,512]{1,0:T(8,128)S(1)} %fusion.4), kind=kOutput, calls=%fused_computation.16 | convolution fusion | flops 1611399168 | bytes 10223616 | tf_op jit(solution)/shard_map/dot_general | solution.py:48
  88.7 0.1 reshape.75
  88.8 0.2 copy.54
  89.1 0.1 reshape.76
  89.2 6.3 %convolution_convert_fusion = bf16[256,6144]{1,0:T(8,128)(2,1)} fusion(bf16[256,512]{1,0:T(8,128)(2,1)S(1)} %reshape.76, bf16[1,512,6144]{2,1,0:T(8,128)(2,1)} %param.25), kind=kOutput, calls=%fused_computation | convolution fusion | flops 1612185600 | bytes 9699328 | tf_op jit(solution)/shard_map/dot_general | solution.py:108
  95.5 0.0 reduce-scatter.2.cloned.1.call-update
  95.6 62.4 %reduce-scatter.2.cloned.1.call-done = bf16[16,6144]{1,0:T(8,128)(2,1)} async-done(((bf16[256,6144]{1,0:T(8,128)(2,1)}), bf16[16,6144]{1,0:T(8,128)(2,1)}) %reduce-scatter.2.cloned.1.call-update) | async-done | bytes 196624 | tf_op jit(solution)/shard_map/reduce_scatter | solution.py:107
  157.9 1.1 all_to_all.19
  159.0 14.8 %all_to_all.25 = bf16[8,2,6144]{2,1,0:T(2,128)(2,1)S(1)} all-to-all(bf16[8,2,6144]{2,1,0:T(2,128)(2,1)S(1)} %all_to_all.19), channel_id=1, replica_groups=mesh['side'=2,'grp'=8,'cuts'=8] {'grp'}, dimensions={0} | all-to-all | bytes 393216 | tf_op jit(solution)/shard_map/all_to_all | solution.py:113
  173.8 0.1 all_to_all.21
  173.9 0.8 fusion
  (7 shorter events, 0.1 us)
Async XLA Ops:
  6.5 5.3 %copy-start = (bf16[4,256,1024]{2,1,0:T(8,128)(2,1)S(1)}, bf16[4,256,1024]{2,1,0:T(8,128)(2,1)}, u32[]{:S(2)}) copy-start(bf16[4,256,1024]{2,1,0:T(8,128)(2,1)} %param.14) | copy-start | bytes 6291460
  6.5 151.4 %reduce-scatter.2.cloned.1.call-start = ((), (), s32[]{:S(2)}) async-start(), calls=%async_computation.3 | async-start | bytes 3342336 | tf_op jit(solution)/shard_map/reduce_scatter | solution.py:107
  11.8 3.1 %copy-start.2 = (bf16[4,6144]{1,0:T(4,128)(2,1)S(1)}, bf16[4,6144]{1,0:T(4,128)(2,1)}, u32[]{:S(2)}) copy-start(bf16[4,6144]{1,0:T(4,128)(2,1)} %param.19) | copy-start | bytes 147460
  11.8 3.4 %copy-start.4 = (bf16[6144,8]{0,1:T(8,128)(2,1)S(1)}, bf16[6144,8]{0,1:T(8,128)(2,1)}, u32[]{:S(2)}) copy-start(bf16[6144,8]{0,1:T(8,128)(2,1)} %param.21) | copy-start | bytes 294916
  11.8 3.6 %copy-start.3 = (s32[4,2]{0,1:T(2,128)S(1)}, s32[4,2]{0,1:T(2,128)}, u32[]{:S(2)}) copy-start(s32[4,2]{0,1:T(2,128)} %param.22) | copy-start | bytes 100
  78.4 5.7 %copy-start.1 = (bf16[256,6144]{1,0:T(8,128)(2,1)S(1)}, bf16[256,6144]{1,0:T(8,128)(2,1)}, u32[]{:S(2)}) copy-start(bf16[256,6144]{1,0:T(8,128)(2,1)} %all_to_all.18) | copy-start | bytes 9437188
Sparse Core Ops, SparseCore 0:
  95.7 62.2 reduce-scatter.1
where the time goes:
time: 182 us
  blocking collectives  67.8 us (37%)
  waiting for transfers between devices  62.4 us (34%)
  matrix products  20.8 us (11%)
  local copies, waits for them, and re-layouts  13.8 us (8%)
  between operations  13.6 us (7%)
  other arithmetic  3.27 us (2%)
    reduce_scatter x1, waiting for transfers between devices, local(): lax.psum_scatter(jnp.dot(hidden, down_w, preferred_element_type=jnp.float...  62.4 us
    all_to_all x1, blocking collectives, local(): lax.all_to_all(copies.reshape(-1, width), ('side', 'grp', 'cuts'), split_...  52.9 us
    all_to_all x1, blocking collectives, local(): lax.all_to_all(mine.astype(jnp.bfloat16), 'grp', split_axis=0, concat_axi...  14.8 us
    all_to_all x1, local copies, waits for them, and re-layouts, local(): lax.all_to_all(copies.reshape(-1, width), ('side', 'grp', 'cuts'), split_...  7.33 us
    dot_general x1, matrix products, local(): jnp.dot(hidden, down_w, preferred_element_type=jnp.float32)  6.34 us
    dot_general x1, matrix products, activate(): gate = jnp.dot(rows_in, gate_w, preferred_element_type=jnp.float32)  5.66 us
    dot_general x1, matrix products, activate(): upper = jnp.dot(rows_in, up_w, preferred_element_type=jnp.float32)  4.68 us
  transfers between devices with their start and end apart: 1, of which 1 were waited for; matrix products, arithmetic and copies ran while one was open for 0% of the time, Pallas kernels for 0%

commit v1 on v0

--- a/solution.py
+++ b/solution.py
@@ -3,11 +3,15 @@
 import jax
 import jax.numpy as jnp
 from jax import lax
+from jax.experimental import pallas as pl
+from jax.experimental.pallas import tpu as pltpu
 from jax.sharding import PartitionSpec as P
 
 Q_HEADS = 48
 KV_HEADS = 8
 HEAD_DIM = 128
+CHUNKS = 8
+MESH = pl.DeviceIdType.MESH
 
 
 def attend(query, k_cache, v_cache, new_key, new_value, lengths):
@@ -43,10 +47,292 @@
     return jnp.sum(same.astype(jnp.int32), axis=1).reshape(block.shape)
 
 
-def activate(rows_in, gate_w, up_w):
-    gate = jnp.dot(rows_in, gate_w, preferred_element_type=jnp.float32)
-    upper = jnp.dot(rows_in, up_w, preferred_element_type=jnp.float32)
-    return (jax.nn.silu(gate) * upper).astype(jnp.bfloat16)
+def expert_kernel(
+    slots, wg_hbm, wu_hbm, wd_hbm, ret,
+    wg, wu, wd, arrived, flat, rows_in, gate, upper, act,
+    own, pair_out, pair_in, raw_out, hop_in, raw_in, sum_out, sum_in, side_out, side_in,
+    back_out, back_in,
+    w_sem, loc_sem, go_send, go_recv, ag_send, ag_recv, rs_send, rs_recv, re_send, re_recv,
+):
+    n, height, width = rows_in.shape
+    half = height // 2
+    heads = slots.shape[1]
+    part = heads // n
+    most = 2
+    experts = lax.axis_size("grp")
+    block = experts * most
+    s, g, c = lax.axis_index("side"), lax.axis_index("grp"), lax.axis_index("cuts")
+    x, core = c // 2, lax.rem(c, 2)
+    other = (1 - s, g, c)
+    right = (s, g, lax.rem(x + 1, 4) * 2 + core)
+    left = (s, g, lax.rem(x + 3, 4) * 2 + core)
+    mate = (s, g, x * 2 + 1 - core)
+
+    def peer(k):
+        return lax.rem(g + k, experts)
+
+    loads = []
+    for i in range(n):
+        loads.append((
+            pltpu.make_async_copy(wg_hbm.at[pl.ds(i * width, width), :], wg.at[i], w_sem.at[0, i]),
+            pltpu.make_async_copy(wu_hbm.at[pl.ds(i * width, width), :], wu.at[i], w_sem.at[1, i]),
+        ))
+    for i in range(n):
+        loads.append((
+            pltpu.make_async_copy(wd_hbm.at[:, pl.ds(i * width, width)], wd.at[i], w_sem.at[2, i]),
+        ))
+    for group in loads:
+        for copy in group:
+            copy.start()
+
+    barrier = pltpu.get_barrier_semaphore()
+    for k in range(1, experts):
+        pl.semaphore_signal(barrier, inc=1, device_id=(s, peer(k), c), device_id_type=MESH)
+    for device in (other, right, left, mate):
+        pl.semaphore_signal(barrier, inc=1, device_id=device, device_id_type=MESH)
+    pl.semaphore_wait(barrier, experts + 3)
+
+    def go(k):
+        return pltpu.make_async_remote_copy(
+            slots.at[pl.ds(peer(k) * most, most)], arrived.at[pl.ds(g * most, most)],
+            go_send.at[k], go_recv.at[k], device_id=(s, peer(k), c), device_id_type=MESH,
+        )
+
+    for k in range(1, experts):
+        go(k).start()
+    mine = pltpu.make_async_copy(
+        slots.at[pl.ds(g * most, most)], arrived.at[pl.ds(g * most, most)], loc_sem.at[0]
+    )
+    mine.start()
+    gate[...] = jnp.zeros_like(gate)
+    upper[...] = jnp.zeros_like(upper)
+    mine.wait()
+    for k in range(1, experts):
+        go(k).wait_recv()
+
+    flat[...] = arrived[...].reshape(block * heads, HEAD_DIM).astype(jnp.float32)
+    for h in range(heads):
+        rows_in[h // part, 0:block, (h % part) * HEAD_DIM:(h % part + 1) * HEAD_DIM] = flat[
+            pl.ds(h, block, stride=heads), :
+        ].astype(jnp.bfloat16)
+
+    table = (
+        (0, 4, other), (0, 3, right), (0, 1, left), (4, 7, right), (4, 5, left), (3, 2, right), (5, 6, left),
+    )
+
+    def ag(i, j):
+        if j == 7:
+            src, dst, device = pl.ds(0, half), pl.ds(half, half), mate
+        else:
+            a, b, device = table[j]
+            src, dst = pl.ds(a * block, block), pl.ds(b * block, block)
+        return pltpu.make_async_remote_copy(
+            rows_in.at[i, src, :], rows_in.at[i, dst, :], ag_send.at[i, j], ag_recv.at[i, j],
+            device_id=device, device_id_type=MESH,
+        )
+
+    def first(i):
+        for j in (0, 1, 2):
+            ag(i, j).start()
+
+    ahead = 3
+    for i in range(ahead):
+        first(i)
+
+    def gather_step(t, carry):
+        @pl.when(t + ahead < n)
+        def _():
+            first(t + ahead)
+
+        @pl.when(t < n)
+        def _():
+            ag(t, 0).wait_recv()
+            ag(t, 3).start()
+            ag(t, 4).start()
+            ag(t, 1).wait_recv()
+            ag(t, 5).start()
+
+        @pl.when((t >= 1) & (t < n + 1))
+        def _():
+            ag(t - 1, 4).wait_recv()
+            ag(t - 1, 6).start()
+
+        @pl.when((t >= 2) & (t < n + 2))
+        def _():
+            for j in (2, 3, 5, 6):
+                ag(t - 2, j).wait_recv()
+            ag(t - 2, 7).start()
+
+        @pl.when(t >= 3)
+        def _():
+            i = t - 3
+            ag(i, 7).wait_recv()
+            pltpu.make_async_copy(wg_hbm.at[pl.ds(0, width), :], wg.at[i], w_sem.at[0, i]).wait()
+            pltpu.make_async_copy(wu_hbm.at[pl.ds(0, width), :], wu.at[i], w_sem.at[1, i]).wait()
+            gate[...] += jnp.dot(rows_in[i], wg[i], preferred_element_type=jnp.float32)
+            upper[...] += jnp.dot(rows_in[i], wu[i], preferred_element_type=jnp.float32)
+
+        return carry
+
+    lax.fori_loop(0, n + 3, gather_step, 0)
+    v = gate[...]
+    act[...] = (v / (1.0 + jnp.exp(-v)) * upper[...]).astype(jnp.bfloat16)
+
+    def rs(i, k):
+        src, dst, device = (
+            (pair_out.at[i], pair_in.at[i], mate),
+            (raw_out.at[i, 0], hop_in.at[i, 0], right),
+            (raw_out.at[i, 1], hop_in.at[i, 1], left),
+            (raw_out.at[i, 2], raw_in.at[i, 0], right),
+            (raw_out.at[i, 3], raw_in.at[i, 1], left),
+            (sum_out.at[i, 0], sum_in.at[i, 0], right),
+            (sum_out.at[i, 1], sum_in.at[i, 1], left),
+            (side_out.at[i], side_in.at[i], other),
+        )[k]
+        return pltpu.make_async_remote_copy(
+            src, dst, rs_send.at[i, k], rs_recv.at[i, k], device_id=device, device_id_type=MESH
+        )
+
+    def of(k):
+        return pl.ds(k * block, block)
+
+    def f32(value):
+        return value.astype(jnp.float32)
+
+    def reduce_step(t, carry):
+        @pl.when(t < n)
+        def _():
+            pltpu.make_async_copy(wd_hbm.at[:, pl.ds(0, width)], wd.at[t], w_sem.at[2, t]).wait()
+            product = jnp.dot(act[...], wd[t], preferred_element_type=jnp.float32)
+            pair_out[t] = product[half:].astype(jnp.bfloat16)
+            own[t] = product[:half]
+            rs(t, 0).start()
+
+        @pl.when((t >= 1) & (t < n + 1))
+        def _():
+            i = t - 1
+            rs(i, 0).wait_recv()
+            total = own[i] + f32(pair_in[i])
+            for place, k in enumerate((2, 6, 5, 3)):
+                raw_out[i, place] = total[k * block:(k + 1) * block].astype(jnp.bfloat16)
+            own[i] = total
+            for k in (1, 2, 3, 4):
+                rs(i, k).start()
+
+        @pl.when((t >= 2) & (t < n + 2))
+        def _():
+            i = t - 2
+            rs(i, 1).wait_recv()
+            sum_out[i, 0] = (own[i, of(1), :] + f32(hop_in[i, 0])).astype(jnp.bfloat16)
+            rs(i, 5).start()
+            rs(i, 2).wait_recv()
+            sum_out[i, 1] = (own[i, of(7), :] + f32(hop_in[i, 1])).astype(jnp.bfloat16)
+            rs(i, 6).start()
+
+        @pl.when((t >= 3) & (t < n + 3))
+        def _():
+            i = t - 3
+            rs(i, 3).wait_recv()
+            rs(i, 6).wait_recv()
+            side_out[i] = (own[i, of(4), :] + f32(raw_in[i, 0]) + f32(sum_in[i, 1])).astype(jnp.bfloat16)
+            rs(i, 7).start()
+
+        @pl.when(t >= 4)
+        def _():
+            i = t - 4
+            for k in (4, 5, 7):
+                rs(i, k).wait_recv()
+            done = own[i, of(0), :] + f32(raw_in[i, 1]) + f32(sum_in[i, 0]) + f32(side_in[i])
+            for h in range(part):
+                flat[pl.ds(i * part + h, block, stride=heads), :] = done[:, h * HEAD_DIM:(h + 1) * HEAD_DIM]
+
+        return carry
+
+    lax.fori_loop(0, n + 4, reduce_step, 0)
+
+    back_out[...] = flat[...].reshape(block, heads, HEAD_DIM).astype(jnp.bfloat16)
+
+    def back(k):
+        return pltpu.make_async_remote_copy(
+            back_out.at[pl.ds(peer(k) * most, most)], back_in.at[pl.ds(g * most, most)],
+            re_send.at[k], re_recv.at[k], device_id=(s, peer(k), c), device_id_type=MESH,
+        )
+
+    for k in range(1, experts):
+        back(k).start()
+    mine = pltpu.make_async_copy(
+        back_out.at[pl.ds(g * most, most)], back_in.at[pl.ds(g * most, most)], loc_sem.at[1]
+    )
+    mine.start()
+
+    def drain(i, carry):
+        for j in range(8):
+            ag(i, j).wait_send()
+            rs(i, j).wait_send()
+        return carry
+
+    lax.fori_loop(0, n, drain, 0)
+    for k in range(1, experts):
+        go(k).wait_send()
+        back(k).wait_send()
+    mine.wait()
+    for k in range(1, experts):
+        back(k).wait_recv()
+    ret[...] = back_in[...]
+
+
+def run_experts(outgoing, gate_w, up_w, down_w):
+    total, heads, _ = outgoing.shape
+    depth, hidden = gate_w.shape
+    n = CHUNKS
+    width = depth // n
+    height = 16 * total
+    half = height // 2
+    bf16, f32 = jnp.bfloat16, jnp.float32
+    dma = pltpu.SemaphoreType.DMA
+    return pl.pallas_call(
+        expert_kernel,
+        out_shape=jax.ShapeDtypeStruct(outgoing.shape, bf16),
+        in_specs=[pl.BlockSpec(memory_space=pltpu.VMEM)] + [pl.BlockSpec(memory_space=pl.ANY)] * 3,
+        out_specs=pl.BlockSpec(memory_space=pltpu.VMEM),
+        scratch_shapes=[
+            pltpu.VMEM((n, width, hidden), bf16),
+            pltpu.VMEM((n, width, hidden), bf16),
+            pltpu.VMEM((n, hidden, width), bf16),
+            pltpu.VMEM(outgoing.shape, bf16),
+            pltpu.VMEM((total * heads, HEAD_DIM), f32),
+            pltpu.VMEM((n, height, width), bf16),
+            pltpu.VMEM((height, hidden), f32),
+            pltpu.VMEM((height, hidden), f32),
+            pltpu.VMEM((height, hidden), bf16),
+            pltpu.VMEM((n, half, width), f32),
+            pltpu.VMEM((n, half, width), bf16),
+            pltpu.VMEM((n, half, width), bf16),
+            pltpu.VMEM((n, 4, total, width), bf16),
+            pltpu.VMEM((n, 2, total, width), bf16),
+            pltpu.VMEM((n, 2, total, width), bf16),
+            pltpu.VMEM((n, 2, total, width), bf16),
+            pltpu.VMEM((n, 2, total, width), bf16),
+            pltpu.VMEM((n, total, width), bf16),
+            pltpu.VMEM((n, total, width), bf16),
+            pltpu.VMEM(outgoing.shape, bf16),
+            pltpu.VMEM(outgoing.shape, bf16),
+            dma((3, n)),
+            dma((2,)),
+            dma((8,)),
+            dma((8,)),
+            dma((n, 8)),
+            dma((n, 8)),
+            dma((n, 8)),
+            dma((n, 8)),
+            dma((8,)),
+            dma((8,)),
+        ],
+        compiler_params=pltpu.CompilerParams(
+            collective_id=0, has_side_effects=True, vmem_limit_bytes=50 * 1024 * 1024
+        ),
+        name="experts",
+    )(outgoing, gate_w, up_w, down_w)
 
 
 def local(
@@ -67,12 +353,7 @@
     rows = query.shape[0]
     width = query.shape[1]
     experts = lax.axis_size("grp")
-    n_side = lax.axis_size("side")
-    n_cuts = lax.axis_size("cuts")
     most = max(2, 2 * rows // experts)
-    gate_w = w_gate[0]
-    up_w = w_up[0]
-    down_w = w_down[0]
     attended = attend(query, k_cache, v_cache, new_key, new_value, lengths)
     mixed = residual.astype(jnp.float32) + attended
     power = jnp.mean(mixed * mixed, axis=1, keepdims=True)
@@ -91,28 +372,10 @@
     outgoing = jnp.einsum("rj,rx->jx", one_hot, normed, preferred_element_type=jnp.float32).astype(
         jnp.bfloat16
     )
-    copies = jnp.broadcast_to(
-        outgoing.reshape(1, experts, 1, most, width), (n_side, experts, n_cuts, most, width)
-    )
-    arrived = lax.all_to_all(
-        copies.reshape(-1, width), ("side", "grp", "cuts"), split_axis=0, concat_axis=0, tiled=True
-    )
-    hidden = activate(arrived, gate_w, up_w)
-    ff_dev = hidden.shape[1]
-    hidden = (
-        hidden.reshape(n_side, experts, n_cuts, most, ff_dev)
-        .transpose(0, 2, 1, 3, 4)
-        .reshape(-1, ff_dev)
-    )
-    mine = lax.psum_scatter(
-        jnp.dot(hidden, down_w, preferred_element_type=jnp.float32).astype(jnp.bfloat16),
-        ("side", "cuts"),
-        scatter_dimension=0,
-        tiled=True,
-    ).astype(jnp.float32)
-    returned = lax.all_to_all(
-        mine.astype(jnp.bfloat16), "grp", split_axis=0, concat_axis=0, tiled=True
-    ).astype(mine.dtype)
+    returned = run_experts(
+        outgoing.reshape(experts * most, Q_HEADS, HEAD_DIM), w_gate[0], w_up[0], w_down[0]
+    )
+    returned = returned.reshape(experts * most, width).astype(jnp.float32)
     mixing = jnp.sum(jnp.where(placing, weights[:, :, None], 0.0), axis=1)
     combined = jnp.dot(
         mixing, returned, precision=lax.Precision.HIGHEST, preferred_element_type=jnp.float32

time: 182 us -> 84.6 us (0.46)
  Pallas kernels: 0 us -> 74.1 us
  blocking collectives: 67.8 us -> 0 us
  waiting for transfers between devices: 62.4 us -> 0 us
  matrix products: 20.8 us -> 2.58 us
  between operations: 13.6 us -> 0.14 us
  local copies, waits for them, and re-layouts: 13.8 us -> 3.15 us
    pallas_call x0 -> x1, Pallas kernels: none -> 74.1 us  [run_experts(): pl.pallas_call(expert_kernel, out_shape=jax.ShapeDtypeStruct(outgoing.sha...]
    all_to_all x2 -> x0, blocking collectives: 67.8 us -> none  [the longest x1 52.9 us: local(): lax.all_to_all(copies.reshape(-1, width), ('side', 'grp', 'cuts'), split_...]
    reduce_scatter x1 -> x0, waiting for transfers between devices: 62.4 us -> none  [local(): lax.psum_scatter(jnp.dot(hidden, down_w, preferred_element_type=jnp.float...]
    dot_general x3 -> x0, matrix products: 16.7 us -> none  [the longest x1 6.34 us: local(): jnp.dot(hidden, down_w, preferred_element_type=jnp.float32)]
    all_to_all x3 -> x0, local copies, waits for them, and re-layouts: 8.47 us -> none  [the longest x1 7.33 us: local(): lax.all_to_all(copies.reshape(-1, width), ('side', 'grp', 'cuts'), split_...]
    broadcast_in_dim x2 -> x0, local copies, waits for them, and re-layouts: 2.14 us -> none  [local(): jnp.broadcast_to(outgoing.reshape(1, experts, 1, most, width), (n_side, e...]
  transfers between devices with their start and end apart: 1 -> 0, of which waited for: 1 -> 0; matrix products, arithmetic and copies ran while one was open for 0% -> 0% of each run, Pallas kernels for 0% -> 0%
where the time goes in v1:
time: 84.6 us; the launch traced here: 83.2 us
  Pallas kernels  74.1 us (88%)
  other arithmetic  3.25 us (4%)
  local copies, waits for them, and re-layouts  3.15 us (4%)
  matrix products  2.58 us (3%)
    pallas_call x1, Pallas kernels, run_experts(): pl.pallas_call(expert_kernel, out_shape=jax.ShapeDtypeStruct(outgoing.sha...  74.1 us

profile of v1, /device:TPU:0, one launch (start us, length us, event | category | flops | bytes accessed | tf_op | source)
XLA Modules:
  0.0 83.2 jit_solution(18282578491306248509)
XLA Ops:
  0.0 0.0 copy-start
  0.0 0.9 %iota_compare_fusion.3 = pred[4,256]{1,0:T(4,128)(4,1)S(1)} fusion(s32[4]{0:T(128)} %param.18), kind=kLoop, calls=%fused_computation.37 | loop fusion | flops 1024 | bytes 1040 | tf_op jit(solution)/shard_map/lt | solution.py:30
  0.9 0.8 copy.26
  1.6 0.1 eq.20
  1.7 0.2 convert_reduce_fusion.1
  1.9 0.1 reshape.66
  2.0 0.1 copy.28
  2.1 0.7 reshape.73
  2.8 0.7 convert_bitcast_fusion
  3.5 0.7 convert_element_type.40
  4.2 0.9 %reshape.61 = bf16[4,8,6,128]{3,2,1,0:T(8,128)(2,1)S(1)} reshape(bf16[4,6144]{1,0:T(4,128)(2,1)} %param.13) | data formatting | bytes 98304 | tf_op jit(solution)/shard_map/reshape | solution.py:21
  5.1 0.0 copy-start.3
  5.1 0.1 fusion.27
  5.3 0.0 copy-done
  5.3 0.7 fusion.26
  6.0 0.0 copy-start.1
  6.0 0.0 copy-start.4
  6.0 0.2 fusion.17
  6.2 0.0 copy-start.2
  6.3 0.4 copy-done.3
  6.7 0.4 fusion.14
  7.1 0.1 reshape.65
  7.2 0.0 copy-done.1
  7.2 0.2 multiply_reduce_fusion
  7.4 0.1 multiply_convert_fusion
  7.5 0.0 copy-done.4
  7.5 0.2 fusion.28
  7.7 0.0 copy-done.2
  7.7 0.2 select_reduce_fusion.1
  7.9 0.1 convert_reduce_fusion
  8.0 0.3 fusion.13
  8.3 74.1 %experts.1 = bf16[16,48,128]{2,1,0:T(8,128)(2,1)S(1)} custom-call(bf16[16,48,128]{2,1,0:T(8,128)(2,1)S(1)} %bitcast.48, bf16[6144,512]{1,0:T(8,128)(2,1)} %bitcast.49, bf16[6144,512]{1,0:T(8,128)(2,1)} %bitcast.50, bf16[512,6144]{1,0:T(8,128)(2,1)} %bitcast.51), custom_call_target="tpu_custom_call" | custom-call | tf_op jit(solution)/shard_map/experts/pallas_call | solution.py:293
  82.4 0.9 %fusion = bf16[4,6144]{1,0:T(4,128)(2,1)} fusion(f32[4,16]{1,0:T(4,128)S(1)} %get-tuple-element.6, bf16[2,8,48,128]{3,2,1,0:T(8,128)(2,1)S(1)} %bitcast.47, f32[4,6144]{1,0:T(4,128)S(1)} %reshape.65, bf16[4,6144]{1,0:T(4,128)(2,1)S(1)} %copy-done.1), kind=kOutput, calls=%fused_computation.2 | convolution fusion | flops 4816896 | bytes 393472 | tf_op jit(solution)/shard_map/dot_general | solution.py:380
  (8 shorter events, 0.1 us)
Async XLA Ops:
  0.0 5.3 %copy-start = (bf16[4,256,1024]{2,1,0:T(8,128)(2,1)S(1)}, bf16[4,256,1024]{2,1,0:T(8,128)(2,1)}, u32[]{:S(2)}) copy-start(bf16[4,256,1024]{2,1,0:T(8,128)(2,1)} %param.14) | copy-start | bytes 6291460
  5.1 1.6 %copy-start.3 = (bf16[4,256,1024]{2,1,0:T(8,128)(2,1)S(1)}, bf16[4,256,1024]{2,1,0:T(8,128)(2,1)}, u32[]{:S(2)}) copy-start(bf16[4,256,1024]{2,1,0:T(8,128)(2,1)} %param.15) | copy-start | bytes 6291460
  6.0 1.2 %copy-start.1 = (bf16[4,6144]{1,0:T(4,128)(2,1)S(1)}, bf16[4,6144]{1,0:T(4,128)(2,1)}, u32[]{:S(2)}) copy-start(bf16[4,6144]{1,0:T(4,128)(2,1)} %param.19) | copy-start | bytes 147460
  6.0 1.5 %copy-start.4 = (bf16[6144,8]{0,1:T(8,128)(2,1)S(1)}, bf16[6144,8]{0,1:T(8,128)(2,1)}, u32[]{:S(2)}) copy-start(bf16[6144,8]{0,1:T(8,128)(2,1)} %param.21) | copy-start | bytes 294916
  6.2 1.4 %copy-start.2 = (s32[4,2]{0,1:T(2,128)S(1)}, s32[4,2]{0,1:T(2,128)}, u32[]{:S(2)}) copy-start(s32[4,2]{0,1:T(2,128)} %param.22) | copy-start | bytes 100

commit v2 on v1

--- a/solution.py
+++ b/solution.py
@@ -152,20 +152,20 @@
             ag(t, 1).wait_recv()
             ag(t, 5).start()
 
-        @pl.when((t >= 1) & (t < n + 1))
-        def _():
-            ag(t - 1, 4).wait_recv()
-            ag(t - 1, 6).start()
-
         @pl.when((t >= 2) & (t < n + 2))
         def _():
+            ag(t - 2, 4).wait_recv()
+            ag(t - 2, 6).start()
+
+        @pl.when((t >= 4) & (t < n + 4))
+        def _():
             for j in (2, 3, 5, 6):
-                ag(t - 2, j).wait_recv()
-            ag(t - 2, 7).start()
-
-        @pl.when(t >= 3)
-        def _():
-            i = t - 3
+                ag(t - 4, j).wait_recv()
+            ag(t - 4, 7).start()
+
+        @pl.when(t >= 5)
+        def _():
+            i = t - 5
             ag(i, 7).wait_recv()
             pltpu.make_async_copy(wg_hbm.at[pl.ds(0, width), :], wg.at[i], w_sem.at[0, i]).wait()
             pltpu.make_async_copy(wu_hbm.at[pl.ds(0, width), :], wu.at[i], w_sem.at[1, i]).wait()
@@ -174,7 +174,7 @@
 
         return carry
 
-    lax.fori_loop(0, n + 3, gather_step, 0)
+    lax.fori_loop(0, n + 5, gather_step, 0)
     v = gate[...]
     act[...] = (v / (1.0 + jnp.exp(-v)) * upper[...]).astype(jnp.bfloat16)
 
@@ -219,9 +219,9 @@
             for k in (1, 2, 3, 4):
                 rs(i, k).start()
 
-        @pl.when((t >= 2) & (t < n + 2))
-        def _():
-            i = t - 2
+        @pl.when((t >= 3) & (t < n + 3))
+        def _():
+            i = t - 3
             rs(i, 1).wait_recv()
             sum_out[i, 0] = (own[i, of(1), :] + f32(hop_in[i, 0])).astype(jnp.bfloat16)
             rs(i, 5).start()
@@ -229,17 +229,17 @@
             sum_out[i, 1] = (own[i, of(7), :] + f32(hop_in[i, 1])).astype(jnp.bfloat16)
             rs(i, 6).start()
 
-        @pl.when((t >= 3) & (t < n + 3))
-        def _():
-            i = t - 3
+        @pl.when((t >= 5) & (t < n + 5))
+        def _():
+            i = t - 5
             rs(i, 3).wait_recv()
             rs(i, 6).wait_recv()
             side_out[i] = (own[i, of(4), :] + f32(raw_in[i, 0]) + f32(sum_in[i, 1])).astype(jnp.bfloat16)
             rs(i, 7).start()
 
-        @pl.when(t >= 4)
-        def _():
-            i = t - 4
+        @pl.when(t >= 7)
+        def _():
+            i = t - 7
             for k in (4, 5, 7):
                 rs(i, k).wait_recv()
             done = own[i, of(0), :] + f32(raw_in[i, 1]) + f32(sum_in[i, 0]) + f32(side_in[i])
@@ -248,7 +248,7 @@
 
         return carry
 
-    lax.fori_loop(0, n + 4, reduce_step, 0)
+    lax.fori_loop(0, n + 7, reduce_step, 0)
 
     back_out[...] = flat[...].reshape(block, heads, HEAD_DIM).astype(jnp.bfloat16)
 

time: 84.6 us -> 71.5 us (0.85)
  Pallas kernels: 74.1 us -> 61.3 us
    pallas_call x1, Pallas kernels: 74.1 us -> 61.3 us  [run_experts(): pl.pallas_call(expert_kernel, out_shape=jax.ShapeDtypeStruct(outgoing.sha...]
where the time goes in v2:
time: 71.5 us; the launch traced here: 70.5 us
  Pallas kernels  61.3 us (86%)
  other arithmetic  3.25 us (5%)
  local copies, waits for them, and re-layouts  3.15 us (4%)
  matrix products  2.58 us (4%)
    pallas_call x1, Pallas kernels, run_experts(): pl.pallas_call(expert_kernel, out_shape=jax.ShapeDtypeStruct(outgoing.sha...  61.3 us

profile of v2, /device:TPU:0, one launch (start us, length us, event | category | flops | bytes accessed | tf_op | source)
XLA Modules:
  0.0 70.5 jit_solution(7832343215244259063)
XLA Ops:
  0.0 0.0 copy-start
  0.0 0.9 %iota_compare_fusion.3 = pred[4,256]{1,0:T(4,128)(4,1)S(1)} fusion(s32[4]{0:T(128)} %param.18), kind=kLoop, calls=%fused_computation.37 | loop fusion | flops 1024 | bytes 1040 | tf_op jit(solution)/shard_map/lt | solution.py:30
  0.9 0.8 %copy.26 = s32[4,2]{1,0:T(4,128)S(1)} copy(s32[4,2]{0,1:T(2,128)} %param.22) | data formatting | bytes 64 | tf_op args[9]
  1.6 0.1 eq.20
  1.7 0.2 convert_reduce_fusion.1
  1.9 0.1 reshape.66
  2.0 0.1 copy.28
  2.1 0.7 %reshape.73 = bf16[4,8,128,1]{2,3,1,0:T(2,128)(2,1)S(1)} reshape(bf16[4,1024]{1,0:T(4,128)(2,1)} %param.16) | data formatting | bytes 16384 | tf_op jit(solution)/shard_map/reshape | solution.py:24
  2.8 0.7 convert_bitcast_fusion
  3.5 0.7 %convert_element_type.40 = f32[6144]{0:T(1024)S(1)} convert(bf16[6144]{0:T(1024)(128)(2,1)} %param.20) | non-fusion elementwise | flops 6144 | bytes 36864 | tf_op jit(solution)/shard_map/convert_element_type | solution.py:360
  4.2 0.9 %reshape.61 = bf16[4,8,6,128]{3,2,1,0:T(8,128)(2,1)S(1)} reshape(bf16[4,6144]{1,0:T(4,128)(2,1)} %param.13) | data formatting | bytes 98304 | tf_op jit(solution)/shard_map/reshape | solution.py:21
  5.1 0.0 copy-start.3
  5.1 0.1 fusion.27
  5.3 0.0 copy-done
  5.3 0.7 %fusion.26 = (f32[4,8,6]{2,1,0:T(8,128)S(1)}, f32[4,8,6,256]{3,2,1,0:T(8,128)S(1)}) fusion(bf16[4,8,6,128]{3,2,1,0:T(8,128)(2,1)S(1)} %reshape.61, pred[4,256]{1,0:T(4,128)(4,1)S(1)} %iota_compare_fusion.3, bf16[4,256,1024]{2,1,0:T(8,128)(2,1)S(1)} %copy-done), kind=kOutput, calls=%fused_computation.45 | convolution fusion | flops 12730176 | bytes 2344704 | tf_op jit(solution)/shard_map/rkgd,rskd->rkgs/dot_general | solution.py:26
  6.0 0.0 copy-start.1
  6.0 0.0 copy-start.4
  6.0 0.2 fusion.17
  6.2 0.0 copy-start.2
  6.3 0.4 copy-done.3
  6.7 0.4 fusion.14
  7.1 0.1 reshape.65
  7.2 0.0 copy-done.1
  7.2 0.2 multiply_reduce_fusion
  7.4 0.1 multiply_convert_fusion
  7.5 0.0 copy-done.4
  7.5 0.2 fusion.28
  7.7 0.0 copy-done.2
  7.7 0.2 select_reduce_fusion.1
  7.9 0.1 convert_reduce_fusion
  8.0 0.3 fusion.13
  8.3 61.3 %experts.1 = bf16[16,48,128]{2,1,0:T(8,128)(2,1)S(1)} custom-call(bf16[16,48,128]{2,1,0:T(8,128)(2,1)S(1)} %bitcast.48, bf16[6144,512]{1,0:T(8,128)(2,1)} %bitcast.49, bf16[6144,512]{1,0:T(8,128)(2,1)} %bitcast.50, bf16[512,6144]{1,0:T(8,128)(2,1)} %bitcast.51), custom_call_target="tpu_custom_call" | custom-call | tf_op jit(solution)/shard_map/experts/pallas_call | solution.py:293
  69.6 0.9 %fusion = bf16[4,6144]{1,0:T(4,128)(2,1)} fusion(f32[4,16]{1,0:T(4,128)S(1)} %get-tuple-element.6, bf16[2,8,48,128]{3,2,1,0:T(8,128)(2,1)S(1)} %bitcast.47, f32[4,6144]{1,0:T(4,128)S(1)} %reshape.65, bf16[4,6144]{1,0:T(4,128)(2,1)S(1)} %copy-done.1), kind=kOutput, calls=%fused_computation.2 | convolution fusion | flops 4816896 | bytes 393472 | tf_op jit(solution)/shard_map/dot_general | solution.py:380
  (8 shorter events, 0.1 us)
Async XLA Ops:
  0.0 5.3 %copy-start = (bf16[4,256,1024]{2,1,0:T(8,128)(2,1)S(1)}, bf16[4,256,1024]{2,1,0:T(8,128)(2,1)}, u32[]{:S(2)}) copy-start(bf16[4,256,1024]{2,1,0:T(8,128)(2,1)} %param.14) | copy-start | bytes 6291460
  5.1 1.6 %copy-start.3 = (bf16[4,256,1024]{2,1,0:T(8,128)(2,1)S(1)}, bf16[4,256,1024]{2,1,0:T(8,128)(2,1)}, u32[]{:S(2)}) copy-start(bf16[4,256,1024]{2,1,0:T(8,128)(2,1)} %param.15) | copy-start | bytes 6291460
  6.0 1.2 %copy-start.1 = (bf16[4,6144]{1,0:T(4,128)(2,1)S(1)}, bf16[4,6144]{1,0:T(4,128)(2,1)}, u32[]{:S(2)}) copy-start(bf16[4,6144]{1,0:T(4,128)(2,1)} %param.19) | copy-start | bytes 147460
  6.0 1.5 %copy-start.4 = (bf16[6144,8]{0,1:T(8,128)(2,1)S(1)}, bf16[6144,8]{0,1:T(8,128)(2,1)}, u32[]{:S(2)}) copy-start(bf16[6144,8]{0,1:T(8,128)(2,1)} %param.21) | copy-start | bytes 294916
  6.2 1.4 %copy-start.2 = (s32[4,2]{0,1:T(2,128)S(1)}, s32[4,2]{0,1:T(2,128)}, u32[]{:S(2)}) copy-start(s32[4,2]{0,1:T(2,128)} %param.22) | copy-start | bytes 100

commit v3 on v2

--- a/solution.py
+++ b/solution.py
@@ -68,6 +68,12 @@
     left = (s, g, lax.rem(x + 3, 4) * 2 + core)
     mate = (s, g, x * 2 + 1 - core)
 
+    def forward(i):
+        return (s, g, lax.rem(x + 1 + 2 * lax.rem(i, 2), 4) * 2 + core)
+
+    def backward(i):
+        return (s, g, lax.rem(x + 3 + 2 * lax.rem(i, 2), 4) * 2 + core)
+
     def peer(k):
         return lax.rem(g + k, experts)
 
@@ -117,12 +123,15 @@
         ].astype(jnp.bfloat16)
 
     table = (
-        (0, 4, other), (0, 3, right), (0, 1, left), (4, 7, right), (4, 5, left), (3, 2, right), (5, 6, left),
+        (0, 4, other), (0, 3, right), (0, 1, left), (4, 7, right), (4, 5, left), None, (2, 6, other),
     )
 
     def ag(i, j):
         if j == 7:
             src, dst, device = pl.ds(0, half), pl.ds(half, half), mate
+        elif j == 5:
+            start = pl.multiple_of((3 - 2 * lax.rem(i, 2)) * block, block)
+            src, dst, device = pl.ds(start, block), pl.ds(2 * block, block), forward(i)
         else:
             a, b, device = table[j]
             src, dst = pl.ds(a * block, block), pl.ds(b * block, block)
@@ -149,17 +158,23 @@
             ag(t, 0).wait_recv()
             ag(t, 3).start()
             ag(t, 4).start()
-            ag(t, 1).wait_recv()
+            pltpu.make_async_copy(
+                rows_in.at[t, 0:block, :], rows_in.at[t, 0:block, :], ag_recv.at[t, 1 + lax.rem(t, 2)]
+            ).wait()
             ag(t, 5).start()
 
         @pl.when((t >= 2) & (t < n + 2))
         def _():
-            ag(t - 2, 4).wait_recv()
+            ag(t - 2, 5).wait_recv()
             ag(t - 2, 6).start()
 
         @pl.when((t >= 4) & (t < n + 4))
         def _():
-            for j in (2, 3, 5, 6):
+            pltpu.make_async_copy(
+                rows_in.at[t - 4, 0:block, :], rows_in.at[t - 4, 0:block, :],
+                ag_recv.at[t - 4, 2 - lax.rem(t, 2)],
+            ).wait()
+            for j in (3, 4, 6):
                 ag(t - 4, j).wait_recv()
             ag(t - 4, 7).start()
 
@@ -181,12 +196,12 @@
     def rs(i, k):
         src, dst, device = (
             (pair_out.at[i], pair_in.at[i], mate),
-            (raw_out.at[i, 0], hop_in.at[i, 0], right),
-            (raw_out.at[i, 1], hop_in.at[i, 1], left),
-            (raw_out.at[i, 2], raw_in.at[i, 0], right),
-            (raw_out.at[i, 3], raw_in.at[i, 1], left),
-            (sum_out.at[i, 0], sum_in.at[i, 0], right),
-            (sum_out.at[i, 1], sum_in.at[i, 1], left),
+            (raw_out.at[i, 0], hop_in.at[i], other),
+            (raw_out.at[i, 1], raw_in.at[i, 0], right),
+            (raw_out.at[i, 2], raw_in.at[i, 1], left),
+            (raw_out.at[i, 3], raw_in.at[i, 2], backward(i)),
+            (sum_out.at[i, 0], sum_in.at[i, 0], forward(i)),
+            (sum_out.at[i, 1], sum_in.at[i, 1], forward(i)),
             (side_out.at[i], side_in.at[i], other),
         )[k]
         return pltpu.make_async_remote_copy(
@@ -213,9 +228,11 @@
             i = t - 1
             rs(i, 0).wait_recv()
             total = own[i] + f32(pair_in[i])
-            for place, k in enumerate((2, 6, 5, 3)):
+            for place, k in enumerate((6, 5, 7)):
                 raw_out[i, place] = total[k * block:(k + 1) * block].astype(jnp.bfloat16)
             own[i] = total
+            near = pl.multiple_of((3 - 2 * lax.rem(i, 2)) * block, block)
+            raw_out[i, 3] = own[i, pl.ds(near, block), :].astype(jnp.bfloat16)
             for k in (1, 2, 3, 4):
                 rs(i, k).start()
 
@@ -223,26 +240,27 @@
         def _():
             i = t - 3
             rs(i, 1).wait_recv()
-            sum_out[i, 0] = (own[i, of(1), :] + f32(hop_in[i, 0])).astype(jnp.bfloat16)
+            sum_out[i, 0] = (own[i, of(2), :] + f32(hop_in[i])).astype(jnp.bfloat16)
             rs(i, 5).start()
             rs(i, 2).wait_recv()
-            sum_out[i, 1] = (own[i, of(7), :] + f32(hop_in[i, 1])).astype(jnp.bfloat16)
+            rs(i, 3).wait_recv()
+            side_out[i] = (own[i, of(4), :] + f32(raw_in[i, 0]) + f32(raw_in[i, 1])).astype(jnp.bfloat16)
+            rs(i, 7).start()
+
+        @pl.when((t >= 5) & (t < n + 5))
+        def _():
+            i = t - 5
+            rs(i, 5).wait_recv()
+            near = pl.multiple_of((1 + 2 * lax.rem(i, 2)) * block, block)
+            sum_out[i, 1] = (own[i, pl.ds(near, block), :] + f32(sum_in[i, 0])).astype(jnp.bfloat16)
             rs(i, 6).start()
 
-        @pl.when((t >= 5) & (t < n + 5))
-        def _():
-            i = t - 5
-            rs(i, 3).wait_recv()
-            rs(i, 6).wait_recv()
-            side_out[i] = (own[i, of(4), :] + f32(raw_in[i, 0]) + f32(sum_in[i, 1])).astype(jnp.bfloat16)
-            rs(i, 7).start()
-
         @pl.when(t >= 7)
         def _():
             i = t - 7
-            for k in (4, 5, 7):
+            for k in (4, 6, 7):
                 rs(i, k).wait_recv()
-            done = own[i, of(0), :] + f32(raw_in[i, 1]) + f32(sum_in[i, 0]) + f32(side_in[i])
+            done = own[i, of(0), :] + f32(raw_in[i, 2]) + f32(sum_in[i, 1]) + f32(side_in[i])
             for h in range(part):
                 flat[pl.ds(i * part + h, block, stride=heads), :] = done[:, h * HEAD_DIM:(h + 1) * HEAD_DIM]
 
@@ -309,8 +327,8 @@
             pltpu.VMEM((n, half, width), bf16),
             pltpu.VMEM((n, half, width), bf16),
             pltpu.VMEM((n, 4, total, width), bf16),
-            pltpu.VMEM((n, 2, total, width), bf16),
-            pltpu.VMEM((n, 2, total, width), bf16),
+            pltpu.VMEM((n, total, width), bf16),
+            pltpu.VMEM((n, 3, total, width), bf16),
             pltpu.VMEM((n, 2, total, width), bf16),
             pltpu.VMEM((n, 2, total, width), bf16),
             pltpu.VMEM((n, total, width), bf16),

time: 71.5 us -> 71.4 us (level)
  no operation moved by 1% of the time
where the time goes in v3:
time: 71.4 us; the launch traced here: 71.1 us
  Pallas kernels  61.9 us (87%)
  other arithmetic  3.25 us (5%)
  local copies, waits for them, and re-layouts  3.15 us (4%)
  matrix products  2.58 us (4%)
    pallas_call x1, Pallas kernels, run_experts(): pl.pallas_call(expert_kernel, out_shape=jax.ShapeDtypeStruct(outgoing.sha...  61.9 us

profile of v3, /device:TPU:0, one launch (start us, length us, event | category | flops | bytes accessed | tf_op | source)
XLA Modules:
  0.0 71.1 jit_solution(11383447365142724728)
XLA Ops:
  0.0 0.0 copy-start
  0.0 0.9 %iota_compare_fusion.3 = pred[4,256]{1,0:T(4,128)(4,1)S(1)} fusion(s32[4]{0:T(128)} %param.18), kind=kLoop, calls=%fused_computation.37 | loop fusion | flops 1024 | bytes 1040 | tf_op jit(solution)/shard_map/lt | solution.py:30
  0.9 0.8 %copy.26 = s32[4,2]{1,0:T(4,128)S(1)} copy(s32[4,2]{0,1:T(2,128)} %param.22) | data formatting | bytes 64 | tf_op args[9]
  1.6 0.1 eq.20
  1.7 0.2 convert_reduce_fusion.1
  1.9 0.1 reshape.66
  2.0 0.1 copy.28
  2.1 0.7 %reshape.73 = bf16[4,8,128,1]{2,3,1,0:T(2,128)(2,1)S(1)} reshape(bf16[4,1024]{1,0:T(4,128)(2,1)} %param.16) | data formatting | bytes 16384 | tf_op jit(solution)/shard_map/reshape | solution.py:24
  2.8 0.7 convert_bitcast_fusion
  3.5 0.7 convert_element_type.40
  4.2 0.9 %reshape.61 = bf16[4,8,6,128]{3,2,1,0:T(8,128)(2,1)S(1)} reshape(bf16[4,6144]{1,0:T(4,128)(2,1)} %param.13) | data formatting | bytes 98304 | tf_op jit(solution)/shard_map/reshape | solution.py:21
  5.1 0.0 copy-start.3
  5.1 0.1 fusion.27
  5.3 0.0 copy-done
  5.3 0.7 %fusion.26 = (f32[4,8,6]{2,1,0:T(8,128)S(1)}, f32[4,8,6,256]{3,2,1,0:T(8,128)S(1)}) fusion(bf16[4,8,6,128]{3,2,1,0:T(8,128)(2,1)S(1)} %reshape.61, pred[4,256]{1,0:T(4,128)(4,1)S(1)} %iota_compare_fusion.3, bf16[4,256,1024]{2,1,0:T(8,128)(2,1)S(1)} %copy-done), kind=kOutput, calls=%fused_computation.45 | convolution fusion | flops 12730176 | bytes 2344704 | tf_op jit(solution)/shard_map/rkgd,rskd->rkgs/dot_general | solution.py:26
  6.0 0.0 copy-start.1
  6.0 0.0 copy-start.4
  6.0 0.2 fusion.17
  6.2 0.0 copy-start.2
  6.3 0.4 copy-done.3
  6.7 0.4 fusion.14
  7.1 0.1 reshape.65
  7.2 0.0 copy-done.1
  7.2 0.2 multiply_reduce_fusion
  7.4 0.1 multiply_convert_fusion
  7.5 0.0 copy-done.4
  7.5 0.2 fusion.28
  7.7 0.0 copy-done.2
  7.7 0.2 select_reduce_fusion.1
  7.9 0.1 convert_reduce_fusion
  8.0 0.3 fusion.13
  8.3 61.9 %experts.1 = bf16[16,48,128]{2,1,0:T(8,128)(2,1)S(1)} custom-call(bf16[16,48,128]{2,1,0:T(8,128)(2,1)S(1)} %bitcast.48, bf16[6144,512]{1,0:T(8,128)(2,1)} %bitcast.49, bf16[6144,512]{1,0:T(8,128)(2,1)} %bitcast.50, bf16[512,6144]{1,0:T(8,128)(2,1)} %bitcast.51), custom_call_target="tpu_custom_call" | custom-call | tf_op jit(solution)/shard_map/experts/pallas_call | solution.py:311
  70.2 0.9 %fusion = bf16[4,6144]{1,0:T(4,128)(2,1)} fusion(f32[4,16]{1,0:T(4,128)S(1)} %get-tuple-element.6, bf16[2,8,48,128]{3,2,1,0:T(8,128)(2,1)S(1)} %bitcast.47, f32[4,6144]{1,0:T(4,128)S(1)} %reshape.65, bf16[4,6144]{1,0:T(4,128)(2,1)S(1)} %copy-done.1), kind=kOutput, calls=%fused_computation.2 | convolution fusion | flops 4816896 | bytes 393472 | tf_op jit(solution)/shard_map/dot_general | solution.py:398
  (8 shorter events, 0.1 us)
Async XLA Ops:
  0.0 5.3 %copy-start = (bf16[4,256,1024]{2,1,0:T(8,128)(2,1)S(1)}, bf16[4,256,1024]{2,1,0:T(8,128)(2,1)}, u32[]{:S(2)}) copy-start(bf16[4,256,1024]{2,1,0:T(8,128)(2,1)} %param.14) | copy-start | bytes 6291460
  5.1 1.6 %copy-start.3 = (bf16[4,256,1024]{2,1,0:T(8,128)(2,1)S(1)}, bf16[4,256,1024]{2,1,0:T(8,128)(2,1)}, u32[]{:S(2)}) copy-start(bf16[4,256,1024]{2,1,0:T(8,128)(2,1)} %param.15) | copy-start | bytes 6291460
  6.0 1.2 %copy-start.1 = (bf16[4,6144]{1,0:T(4,128)(2,1)S(1)}, bf16[4,6144]{1,0:T(4,128)(2,1)}, u32[]{:S(2)}) copy-start(bf16[4,6144]{1,0:T(4,128)(2,1)} %param.19) | copy-start | bytes 147460
  6.0 1.5 %copy-start.4 = (bf16[6144,8]{0,1:T(8,128)(2,1)S(1)}, bf16[6144,8]{0,1:T(8,128)(2,1)}, u32[]{:S(2)}) copy-start(bf16[6144,8]{0,1:T(8,128)(2,1)} %param.21) | copy-start | bytes 294916
  6.2 1.4 %copy-start.2 = (s32[4,2]{0,1:T(2,128)S(1)}, s32[4,2]{0,1:T(2,128)}, u32[]{:S(2)}) copy-start(s32[4,2]{0,1:T(2,128)} %param.22) | copy-start | bytes 100

commit v4 on v3

--- a/solution.py
+++ b/solution.py
@@ -10,7 +10,8 @@
 Q_HEADS = 48
 KV_HEADS = 8
 HEAD_DIM = 128
-CHUNKS = 8
+CHUNKS = 12
+PARTS = 3
 MESH = pl.DeviceIdType.MESH
 
 
@@ -61,6 +62,7 @@
     most = 2
     experts = lax.axis_size("grp")
     block = experts * most
+    span = heads // PARTS
     s, g, c = lax.axis_index("side"), lax.axis_index("grp"), lax.axis_index("cuts")
     x, core = c // 2, lax.rem(c, 2)
     other = (1 - s, g, c)
@@ -98,14 +100,16 @@
         pl.semaphore_signal(barrier, inc=1, device_id=device, device_id_type=MESH)
     pl.semaphore_wait(barrier, experts + 3)
 
-    def go(k):
+    def go(k, p):
         return pltpu.make_async_remote_copy(
-            slots.at[pl.ds(peer(k) * most, most)], arrived.at[pl.ds(g * most, most)],
-            go_send.at[k], go_recv.at[k], device_id=(s, peer(k), c), device_id_type=MESH,
+            slots.at[pl.ds(peer(k) * most, most), pl.ds(p * span, span)],
+            arrived.at[pl.ds(g * most, most), pl.ds(p * span, span)],
+            go_send.at[p, k], go_recv.at[p, k], device_id=(s, peer(k), c), device_id_type=MESH,
         )
 
-    for k in range(1, experts):
-        go(k).start()
+    for p in range(PARTS):
+        for k in range(1, experts):
+            go(k, p).start()
     mine = pltpu.make_async_copy(
         slots.at[pl.ds(g * most, most)], arrived.at[pl.ds(g * most, most)], loc_sem.at[0]
     )
@@ -113,14 +117,20 @@
     gate[...] = jnp.zeros_like(gate)
     upper[...] = jnp.zeros_like(upper)
     mine.wait()
-    for k in range(1, experts):
-        go(k).wait_recv()
-
-    flat[...] = arrived[...].reshape(block * heads, HEAD_DIM).astype(jnp.float32)
-    for h in range(heads):
-        rows_in[h // part, 0:block, (h % part) * HEAD_DIM:(h % part + 1) * HEAD_DIM] = flat[
-            pl.ds(h, block, stride=heads), :
-        ].astype(jnp.bfloat16)
+
+    def unpack(p):
+        for k in range(1, experts):
+            go(k, p).wait_recv()
+        first_row = p * block * span
+        flat[first_row:first_row + block * span, :] = (
+            arrived[:, p * span:(p + 1) * span, :].astype(jnp.float32).reshape(block * span, HEAD_DIM)
+        )
+        for h in range(p * span, (p + 1) * span):
+            rows_in[h // part, 0:block, (h % part) * HEAD_DIM:(h % part + 1) * HEAD_DIM] = flat[
+                pl.ds(first_row + h % span, block, stride=span), :
+            ].astype(jnp.bfloat16)
+
+    unpack(0)
 
     table = (
         (0, 4, other), (0, 3, right), (0, 1, left), (4, 7, right), (4, 5, left), None, (2, 6, other),
@@ -149,6 +159,11 @@
         first(i)
 
     def gather_step(t, carry):
+        for p in range(1, PARTS):
+            @pl.when(t + ahead == p * span // part)
+            def _(p=p):
+                unpack(p)
+
         @pl.when(t + ahead < n)
         def _():
             first(t + ahead)
@@ -214,6 +229,13 @@
     def f32(value):
         return value.astype(jnp.float32)
 
+    def back(k, p):
+        return pltpu.make_async_remote_copy(
+            back_out.at[pl.ds(peer(k) * most, most), pl.ds(p * span, span)],
+            back_in.at[pl.ds(g * most, most), pl.ds(p * span, span)],
+            re_send.at[p, k], re_recv.at[p, k], device_id=(s, peer(k), c), device_id_type=MESH,
+        )
+
     def reduce_step(t, carry):
         @pl.when(t < n)
         def _():
@@ -261,23 +283,23 @@
             for k in (4, 6, 7):
                 rs(i, k).wait_recv()
             done = own[i, of(0), :] + f32(raw_in[i, 2]) + f32(sum_in[i, 1]) + f32(side_in[i])
+            chunks = span // part
+            place = (i // chunks) * (block * span) + lax.rem(i, chunks) * part
             for h in range(part):
-                flat[pl.ds(i * part + h, block, stride=heads), :] = done[:, h * HEAD_DIM:(h + 1) * HEAD_DIM]
+                flat[pl.ds(place + h, block, stride=span), :] = done[:, h * HEAD_DIM:(h + 1) * HEAD_DIM]
+            for p in range(PARTS):
+                @pl.when(i == (p + 1) * chunks - 1)
+                def _(p=p):
+                    back_out[:, p * span:(p + 1) * span, :] = (
+                        flat[p * block * span:(p + 1) * block * span, :]
+                        .reshape(block, span, HEAD_DIM).astype(jnp.bfloat16)
+                    )
+                    for k in range(1, experts):
+                        back(k, p).start()
 
         return carry
 
     lax.fori_loop(0, n + 7, reduce_step, 0)
-
-    back_out[...] = flat[...].reshape(block, heads, HEAD_DIM).astype(jnp.bfloat16)
-
-    def back(k):
-        return pltpu.make_async_remote_copy(
-            back_out.at[pl.ds(peer(k) * most, most)], back_in.at[pl.ds(g * most, most)],
-            re_send.at[k], re_recv.at[k], device_id=(s, peer(k), c), device_id_type=MESH,
-        )
-
-    for k in range(1, experts):
-        back(k).start()
     mine = pltpu.make_async_copy(
         back_out.at[pl.ds(g * most, most)], back_in.at[pl.ds(g * most, most)], loc_sem.at[1]
     )
@@ -290,12 +312,14 @@
         return carry
 
     lax.fori_loop(0, n, drain, 0)
-    for k in range(1, experts):
-        go(k).wait_send()
-        back(k).wait_send()
+    for p in range(PARTS):
+        for k in range(1, experts):
+            go(k, p).wait_send()
+            back(k, p).wait_send()
     mine.wait()
-    for k in range(1, experts):
-        back(k).wait_recv()
+    for p in range(PARTS):
+        for k in range(1, experts):
+            back(k, p).wait_recv()
     ret[...] = back_in[...]
 
 
@@ -337,14 +361,14 @@
             pltpu.VMEM(outgoing.shape, bf16),
             dma((3, n)),
             dma((2,)),
-            dma((8,)),
-            dma((8,)),
+            dma((PARTS, 8)),
+            dma((PARTS, 8)),
             dma((n, 8)),
             dma((n, 8)),
             dma((n, 8)),
             dma((n, 8)),
-            dma((8,)),
-            dma((8,)),
+            dma((PARTS, 8)),
+            dma((PARTS, 8)),
         ],
         compiler_params=pltpu.CompilerParams(
             collective_id=0, has_side_effects=True, vmem_limit_bytes=50 * 1024 * 1024

time: 71.4 us -> 81.3 us (1.14)
  Pallas kernels: 61.9 us -> 71.9 us
    pallas_call x1, Pallas kernels: 61.9 us -> 71.9 us  [run_experts(): pl.pallas_call(expert_kernel, out_shape=jax.ShapeDtypeStruct(outgoing.sha...]
where the time goes in v4:
time: 81.3 us; the launch traced here: 81 us
  Pallas kernels  71.9 us (88%)
  other arithmetic  3.25 us (4%)
  local copies, waits for them, and re-layouts  3.15 us (4%)
  matrix products  2.58 us (3%)
    pallas_call x1, Pallas kernels, run_experts(): pl.pallas_call(expert_kernel, out_shape=jax.ShapeDtypeStruct(outgoing.sha...  71.9 us

profile of v4, /device:TPU:0, one launch (start us, length us, event | category | flops | bytes accessed | tf_op | source)
XLA Modules:
  0.0 81.0 jit_solution(2906793627457322728)
XLA Ops:
  0.0 0.0 copy-start
  0.0 0.9 %iota_compare_fusion.3 = pred[4,256]{1,0:T(4,128)(4,1)S(1)} fusion(s32[4]{0:T(128)} %param.18), kind=kLoop, calls=%fused_computation.37 | loop fusion | flops 1024 | bytes 1040 | tf_op jit(solution)/shard_map/lt | solution.py:31
  0.9 0.8 copy.26
  1.6 0.1 eq.20
  1.7 0.2 convert_reduce_fusion.1
  1.9 0.1 reshape.66
  2.0 0.1 copy.28
  2.1 0.7 reshape.73
  2.8 0.7 convert_bitcast_fusion
  3.5 0.7 convert_element_type.40
  4.2 0.9 %reshape.61 = bf16[4,8,6,128]{3,2,1,0:T(8,128)(2,1)S(1)} reshape(bf16[4,6144]{1,0:T(4,128)(2,1)} %param.13) | data formatting | bytes 98304 | tf_op jit(solution)/shard_map/reshape | solution.py:22
  5.1 0.0 copy-start.3
  5.1 0.1 fusion.27
  5.3 0.0 copy-done
  5.3 0.7 fusion.26
  6.0 0.0 copy-start.1
  6.0 0.0 copy-start.4
  6.0 0.2 fusion.17
  6.2 0.0 copy-start.2
  6.3 0.4 copy-done.3
  6.7 0.4 fusion.14
  7.1 0.1 reshape.65
  7.2 0.0 copy-done.1
  7.2 0.2 multiply_reduce_fusion
  7.4 0.1 multiply_convert_fusion
  7.5 0.0 copy-done.4
  7.5 0.2 fusion.28
  7.7 0.0 copy-done.2
  7.7 0.2 select_reduce_fusion.1
  7.9 0.1 convert_reduce_fusion
  8.0 0.3 fusion.13
  8.3 71.9 %experts.1 = bf16[16,48,128]{2,1,0:T(8,128)(2,1)S(1)} custom-call(bf16[16,48,128]{2,1,0:T(8,128)(2,1)S(1)} %bitcast.48, bf16[6144,512]{1,0:T(8,128)(2,1)} %bitcast.49, bf16[6144,512]{1,0:T(8,128)(2,1)} %bitcast.50, bf16[512,6144]{1,0:T(8,128)(2,1)} %bitcast.51), custom_call_target="tpu_custom_call" | custom-call | tf_op jit(solution)/shard_map/experts/pallas_call | solution.py:335
  80.1 0.9 %fusion = bf16[4,6144]{1,0:T(4,128)(2,1)} fusion(f32[4,16]{1,0:T(4,128)S(1)} %get-tuple-element.6, bf16[2,8,48,128]{3,2,1,0:T(8,128)(2,1)S(1)} %bitcast.47, f32[4,6144]{1,0:T(4,128)S(1)} %reshape.65, bf16[4,6144]{1,0:T(4,128)(2,1)S(1)} %copy-done.1), kind=kOutput, calls=%fused_computation.2 | convolution fusion | flops 4816896 | bytes 393472 | tf_op jit(solution)/shard_map/dot_general | solution.py:422
  (8 shorter events, 0.1 us)
Async XLA Ops:
  0.0 5.3 %copy-start = (bf16[4,256,1024]{2,1,0:T(8,128)(2,1)S(1)}, bf16[4,256,1024]{2,1,0:T(8,128)(2,1)}, u32[]{:S(2)}) copy-start(bf16[4,256,1024]{2,1,0:T(8,128)(2,1)} %param.14) | copy-start | bytes 6291460
  5.1 1.6 %copy-start.3 = (bf16[4,256,1024]{2,1,0:T(8,128)(2,1)S(1)}, bf16[4,256,1024]{2,1,0:T(8,128)(2,1)}, u32[]{:S(2)}) copy-start(bf16[4,256,1024]{2,1,0:T(8,128)(2,1)} %param.15) | copy-start | bytes 6291460
  6.0 1.2 %copy-start.1 = (bf16[4,6144]{1,0:T(4,128)(2,1)S(1)}, bf16[4,6144]{1,0:T(4,128)(2,1)}, u32[]{:S(2)}) copy-start(bf16[4,6144]{1,0:T(4,128)(2,1)} %param.19) | copy-start | bytes 147460
  6.0 1.5 %copy-start.4 = (bf16[6144,8]{0,1:T(8,128)(2,1)S(1)}, bf16[6144,8]{0,1:T(8,128)(2,1)}, u32[]{:S(2)}) copy-start(bf16[6144,8]{0,1:T(8,128)(2,1)} %param.21) | copy-start | bytes 294916
  6.2 1.4 %copy-start.2 = (s32[4,2]{0,1:T(2,128)S(1)}, s32[4,2]{0,1:T(2,128)}, u32[]{:S(2)}) copy-start(s32[4,2]{0,1:T(2,128)} %param.22) | copy-start | bytes 100

commit v5 on v4

--- a/solution.py
+++ b/solution.py
@@ -10,7 +10,7 @@
 Q_HEADS = 48
 KV_HEADS = 8
 HEAD_DIM = 128
-CHUNKS = 12
+CHUNKS = 8
 PARTS = 3
 MESH = pl.DeviceIdType.MESH
 
@@ -154,7 +154,7 @@
         for j in (0, 1, 2):
             ag(i, j).start()
 
-    ahead = 3
+    ahead = 2
     for i in range(ahead):
         first(i)
 
@@ -283,12 +283,12 @@
             for k in (4, 6, 7):
                 rs(i, k).wait_recv()
             done = own[i, of(0), :] + f32(raw_in[i, 2]) + f32(sum_in[i, 1]) + f32(side_in[i])
-            chunks = span // part
-            place = (i // chunks) * (block * span) + lax.rem(i, chunks) * part
             for h in range(part):
-                flat[pl.ds(place + h, block, stride=span), :] = done[:, h * HEAD_DIM:(h + 1) * HEAD_DIM]
+                head = i * part + h
+                place = lax.div(head, span) * (block * span) + lax.rem(head, span)
+                flat[pl.ds(place, block, stride=span), :] = done[:, h * HEAD_DIM:(h + 1) * HEAD_DIM]
             for p in range(PARTS):
-                @pl.when(i == (p + 1) * chunks - 1)
+                @pl.when(i == ((p + 1) * span - 1) // part)
                 def _(p=p):
                     back_out[:, p * span:(p + 1) * span, :] = (
                         flat[p * block * span:(p + 1) * block * span, :]

time: 81.3 us -> 71.4 us (0.88)
  Pallas kernels: 71.9 us -> 62 us
    pallas_call x1, Pallas kernels: 71.9 us -> 62 us  [run_experts(): pl.pallas_call(expert_kernel, out_shape=jax.ShapeDtypeStruct(outgoing.sha...]
where the time goes in v5:
time: 71.4 us; the launch traced here: 71.1 us
  Pallas kernels  62 us (87%)
  other arithmetic  3.25 us (5%)
  local copies, waits for them, and re-layouts  3.15 us (4%)
  matrix products  2.58 us (4%)
    pallas_call x1, Pallas kernels, run_experts(): pl.pallas_call(expert_kernel, out_shape=jax.ShapeDtypeStruct(outgoing.sha...  62 us

profile of v5, /device:TPU:0, one launch (start us, length us, event | category | flops | bytes accessed | tf_op | source)
XLA Modules:
  0.0 71.1 jit_solution(3877365839281259181)
XLA Ops:
  0.0 0.0 copy-start
  0.0 0.9 %iota_compare_fusion.3 = pred[4,256]{1,0:T(4,128)(4,1)S(1)} fusion(s32[4]{0:T(128)} %param.18), kind=kLoop, calls=%fused_computation.37 | loop fusion | flops 1024 | bytes 1040 | tf_op jit(solution)/shard_map/lt | solution.py:31
  0.9 0.8 %copy.26 = s32[4,2]{1,0:T(4,128)S(1)} copy(s32[4,2]{0,1:T(2,128)} %param.22) | data formatting | bytes 64 | tf_op args[9]
  1.6 0.1 eq.20
  1.7 0.2 convert_reduce_fusion.1
  1.9 0.1 reshape.66
  2.0 0.1 copy.28
  2.1 0.7 %reshape.73 = bf16[4,8,128,1]{2,3,1,0:T(2,128)(2,1)S(1)} reshape(bf16[4,1024]{1,0:T(4,128)(2,1)} %param.16) | data formatting | bytes 16384 | tf_op jit(solution)/shard_map/reshape | solution.py:25
  2.8 0.7 convert_bitcast_fusion
  3.5 0.7 convert_element_type.40
  4.2 0.9 %reshape.61 = bf16[4,8,6,128]{3,2,1,0:T(8,128)(2,1)S(1)} reshape(bf16[4,6144]{1,0:T(4,128)(2,1)} %param.13) | data formatting | bytes 98304 | tf_op jit(solution)/shard_map/reshape | solution.py:22
  5.1 0.0 copy-start.3
  5.1 0.1 fusion.27
  5.3 0.0 copy-done
  5.3 0.7 %fusion.26 = (f32[4,8,6]{2,1,0:T(8,128)S(1)}, f32[4,8,6,256]{3,2,1,0:T(8,128)S(1)}) fusion(bf16[4,8,6,128]{3,2,1,0:T(8,128)(2,1)S(1)} %reshape.61, pred[4,256]{1,0:T(4,128)(4,1)S(1)} %iota_compare_fusion.3, bf16[4,256,1024]{2,1,0:T(8,128)(2,1)S(1)} %copy-done), kind=kOutput, calls=%fused_computation.45 | convolution fusion | flops 12730176 | bytes 2344704 | tf_op jit(solution)/shard_map/rkgd,rskd->rkgs/dot_general | solution.py:27
  6.0 0.0 copy-start.1
  6.0 0.0 copy-start.4
  6.0 0.2 fusion.17
  6.2 0.0 copy-start.2
  6.3 0.4 copy-done.3
  6.7 0.4 fusion.14
  7.1 0.1 reshape.65
  7.2 0.0 copy-done.1
  7.2 0.2 multiply_reduce_fusion
  7.4 0.1 multiply_convert_fusion
  7.5 0.0 copy-done.4
  7.5 0.2 fusion.28
  7.7 0.0 copy-done.2
  7.7 0.2 select_reduce_fusion.1
  7.9 0.1 convert_reduce_fusion
  8.0 0.3 fusion.13
  8.3 62.0 %experts.1 = bf16[16,48,128]{2,1,0:T(8,128)(2,1)S(1)} custom-call(bf16[16,48,128]{2,1,0:T(8,128)(2,1)S(1)} %bitcast.48, bf16[6144,512]{1,0:T(8,128)(2,1)} %bitcast.49, bf16[6144,512]{1,0:T(8,128)(2,1)} %bitcast.50, bf16[512,6144]{1,0:T(8,128)(2,1)} %bitcast.51), custom_call_target="tpu_custom_call" | custom-call | tf_op jit(solution)/shard_map/experts/pallas_call | solution.py:335
  70.2 0.9 %fusion = bf16[4,6144]{1,0:T(4,128)(2,1)} fusion(f32[4,16]{1,0:T(4,128)S(1)} %get-tuple-element.6, bf16[2,8,48,128]{3,2,1,0:T(8,128)(2,1)S(1)} %bitcast.47, f32[4,6144]{1,0:T(4,128)S(1)} %reshape.65, bf16[4,6144]{1,0:T(4,128)(2,1)S(1)} %copy-done.1), kind=kOutput, calls=%fused_computation.2 | convolution fusion | flops 4816896 | bytes 393472 | tf_op jit(solution)/shard_map/dot_general | solution.py:422
  (8 shorter events, 0.1 us)
Async XLA Ops:
  0.0 5.3 %copy-start = (bf16[4,256,1024]{2,1,0:T(8,128)(2,1)S(1)}, bf16[4,256,1024]{2,1,0:T(8,128)(2,1)}, u32[]{:S(2)}) copy-start(bf16[4,256,1024]{2,1,0:T(8,128)(2,1)} %param.14) | copy-start | bytes 6291460
  5.1 1.6 %copy-start.3 = (bf16[4,256,1024]{2,1,0:T(8,128)(2,1)S(1)}, bf16[4,256,1024]{2,1,0:T(8,128)(2,1)}, u32[]{:S(2)}) copy-start(bf16[4,256,1024]{2,1,0:T(8,128)(2,1)} %param.15) | copy-start | bytes 6291460
  6.0 1.2 %copy-start.1 = (bf16[4,6144]{1,0:T(4,128)(2,1)S(1)}, bf16[4,6144]{1,0:T(4,128)(2,1)}, u32[]{:S(2)}) copy-start(bf16[4,6144]{1,0:T(4,128)(2,1)} %param.19) | copy-start | bytes 147460
  6.0 1.5 %copy-start.4 = (bf16[6144,8]{0,1:T(8,128)(2,1)S(1)}, bf16[6144,8]{0,1:T(8,128)(2,1)}, u32[]{:S(2)}) copy-start(bf16[6144,8]{0,1:T(8,128)(2,1)} %param.21) | copy-start | bytes 294916
  6.2 1.4 %copy-start.2 = (s32[4,2]{0,1:T(2,128)S(1)}, s32[4,2]{0,1:T(2,128)}, u32[]{:S(2)}) copy-start(s32[4,2]{0,1:T(2,128)} %param.22) | copy-start | bytes 100
